TPU v7x, 32 devices: a whole 2x2x4 slice. The times are simulated.
32 devices in a mesh: groups: 2 (over y), seq: 16 (over z, x, core).
Axes of the slice: x: 2, y: 2, z: 4, core: 2. Of those that a mesh axis runs over, the one named last changes fastest.
Arguments:
- queries: bfloat16 [4096, 3072], P(('groups', 'seq')), parts along dimension 0, may hold values from -8 to 8
- keys: bfloat16 [4096, 3072], P(('groups', 'seq')), parts along dimension 0, may hold values from -6 to 6
- values: bfloat16 [4096, 3072], P(('groups', 'seq')), parts along dimension 0, may hold values from -6 to 6
- rand_blocks: int32 [32, 3], P('groups'), parts along dimension 0, may hold values from 0 to 15, as said below
- global_ids: int32 [4], P('groups'), parts along dimension 0, may hold values from 0 to 15, as said below
Outputs:
- attended: bfloat16 [4096, 3072], P(('groups', 'seq')), parts along dimension 0
There are 2 independent parts, one for each index of `groups`. A program takes and returns all parts, laid end to end along the dimension named above; each array names one. Nothing has to cross between parts.
Inputs may be any that keep to these rules, and one draw needn't show every extreme that they name: `rand_blocks`: row b names 3 different blocks, none of them b-1, b, b+1 or a global block. `global_ids`: 2 different blocks, one of which is the last block.
All inputs are finite; a program needn't handle non-finite values.
Results may differ from a plain program's by a relative error of at most 0.0049.
Values may be sent and summed in bfloat16 or wider, within the bound.
A program may use at most 128 MiB of HBM per device.

v0:
```python
from functools import reduce

import jax
import jax.numpy as jnp
from jax import lax
from jax.sharding import PartitionSpec as P

HEADS = 24
HEAD_DIM = 128
BLOCK = 128
GLOBALS = 2
RANDOMS = 3


def padded_2(cells, sides, width):
    for axis, dim in sides:
        count = lax.axis_size(axis)
        ends = count - 1
        head = lax.slice_in_dim(cells, 0, width, axis=dim)
        tail = lax.slice_in_dim(cells, cells.shape[dim] - width, cells.shape[dim], axis=dim)
        cells = jnp.concatenate(
            [
                lax.ppermute(tail, axis, [(i, (i + 1) % count) for i in range(ends)]),
                cells,
                lax.ppermute(head, axis, [((i + 1) % count, i) for i in range(ends)]),
            ],
            axis=dim,
        )
    return cells


def broadcast(array, axis, root):
    mine = lax.axis_index(axis) == root
    return lax.psum(jnp.where(mine, array, jnp.zeros_like(array)), axis)


def is_global(block_ids, global_ids):
    return jnp.any(block_ids[:, None] == global_ids[None, :], axis=1)


def local_scores(query_blocks, key_part, usable, scale):
    scores = (
        jnp.einsum("bqhd,bkhd->bhqk", query_blocks, key_part, preferred_element_type=jnp.float32)
        * scale
    )
    return jnp.where(usable[:, None, None, None], scores, -1e30)


def combine_parts(entries):
    maxima = [jnp.max(scores, axis=tuple(range(3, scores.ndim))) for scores, _, _ in entries]
    top = reduce(jnp.maximum, maxima)
    powers = [
        jnp.exp(scores - jnp.expand_dims(top, tuple(range(3, scores.ndim))))
        for scores, _, _ in entries
    ]
    total = reduce(jnp.add, [jnp.sum(power, axis=tuple(range(3, power.ndim))) for power in powers])
    pieces = []
    for power, entry in zip(powers, entries):
        probs = (power / jnp.expand_dims(total, tuple(range(3, power.ndim)))).astype(jnp.bfloat16)
        pieces.append(jnp.einsum(entry[2], probs, entry[1], preferred_element_type=jnp.float32))
    return reduce(jnp.add, pieces)


def local(queries, keys, values, rand_blocks, global_ids):
    length, width = queries.shape
    blocks_here = length // BLOCK
    block_count = rand_blocks.shape[0]
    scale = HEAD_DIM ** (-0.5)
    my_index = lax.axis_index("seq")
    block_ids = my_index * blocks_here + jnp.arange(blocks_here, dtype=jnp.int32)
    query_blocks = queries.reshape(blocks_here, BLOCK, HEADS, HEAD_DIM)
    near_keys = keys.reshape(blocks_here, BLOCK, HEADS, HEAD_DIM)
    near_values = values.reshape(blocks_here, BLOCK, HEADS, HEAD_DIM)
    stacked = jnp.stack([keys, values])
    key_slab, value_slab = (
        lax.all_to_all(keys.T, "seq", split_axis=0, concat_axis=1, tiled=True),
        lax.all_to_all(values.T, "seq", split_axis=0, concat_axis=1, tiled=True),
    )
    slab_width = key_slab.shape[0]
    key_slab = key_slab.reshape(slab_width, block_count, BLOCK)
    value_slab = value_slab.reshape(slab_width, block_count, BLOCK)
    prev_ok = (block_ids >= 1) & jnp.logical_not(is_global(block_ids - 1, global_ids))
    next_ok = (block_ids + 1 < block_count) & jnp.logical_not(is_global(block_ids + 1, global_ids))
    own_ok = jnp.logical_not(is_global(block_ids, global_ids))
    far_ok = jnp.ones((blocks_here, RANDOMS), dtype=bool)
    slots = rand_blocks.shape[1]
    picked_keys = jnp.take(key_slab, rand_blocks, axis=1)
    picked_values = jnp.take(value_slab, rand_blocks, axis=1)
    fetched_keys, fetched_values = (
        lax.all_to_all(picked_keys, "seq", split_axis=1, concat_axis=0, tiled=True),
        lax.all_to_all(picked_values, "seq", split_axis=1, concat_axis=0, tiled=True),
    )
    far_keys = fetched_keys.reshape(HEADS, HEAD_DIM, blocks_here, slots, BLOCK)
    far_values = fetched_values.reshape(HEADS, HEAD_DIM, blocks_here, slots, BLOCK)
    entries = [
        (local_scores(query_blocks, near_keys, own_ok, scale), near_values, "bhqk,bkhd->bqhd")
    ]
    far_scores = (
        jnp.einsum("bqhd,hdbsk->bhqsk", query_blocks, far_keys, preferred_element_type=jnp.float32)
        * scale
    )
    far_scores = jnp.where(far_ok[:, None, None, :, None], far_scores, -1e30)
    entries.append((far_scores, far_values, "bhqsk,hdbsk->bqhd"))
    padded = padded_2(stacked, (("seq", 1),), BLOCK)
    edge_blocks = padded.reshape(2, blocks_here + 2, BLOCK, HEADS, HEAD_DIM)
    entries.append(
        (
            local_scores(query_blocks, edge_blocks[0, :blocks_here], prev_ok, scale),
            edge_blocks[1, :blocks_here],
            "bhqk,bkhd->bqhd",
        )
    )
    entries.append(
        (
            local_scores(query_blocks, edge_blocks[0, 2:], next_ok, scale),
            edge_blocks[1, 2:],
            "bhqk,bkhd->bqhd",
        )
    )
    panels = []
    for slot_index in range(GLOBALS):
        chosen = global_ids[slot_index]
        panels.append(broadcast(stacked, "seq", chosen // blocks_here))
    panel = jnp.stack(panels)
    global_keys = panel[:, 0].reshape(GLOBALS, BLOCK, HEADS, HEAD_DIM)
    global_values = panel[:, 1].reshape(GLOBALS, BLOCK, HEADS, HEAD_DIM)
    global_scores = (
        jnp.einsum(
            "bqhd,gkhd->bhqgk", query_blocks, global_keys, preferred_element_type=jnp.float32
        )
        * scale
    )
    entries.append((global_scores, global_values, "bhqgk,gkhd->bqhd"))
    result = combine_parts(entries)
    return result.reshape(length, width).astype(jnp.bfloat16)


def solution(mesh):
    placed = (
        P(("groups", "seq"), None),
        P(("groups", "seq"), None),
        P(("groups", "seq"), None),
        P("groups", None),
        P("groups"),
    )
    return jax.shard_map(
        local, mesh=mesh, in_specs=placed, out_specs=P(("groups", "seq"), None), check_vma=False
    )
```

profile of v0, /device:TPU:0, one launch (start us, length us, event | category | flops | bytes accessed | tf_op | source)
XLA Modules:
  0.0 294.5 jit_solution(17898825059002964823)
XLA Ops:
  6.5 2.4 copy.38
  8.9 7.4 %all-to-all-start.2 = ((bf16[16,192,128]{2,1,0:T(8,128)(2,1)}), bf16[16,192,128]{2,1,0:T(8,128)(2,1)S(1)}, u32[]{:S(2)}, u32[]{:S(2)}) async-start(bf16[16,192,128]{2,1,0:T(8,128)(2,1)} %bitcast.29), calls=%async_computation.2 | async-start | bytes 1572864 | tf_op jit(solution)/shard_map/all_to_all | solution.py:77
  16.3 0.0 copy-done.4
  16.3 0.0 copy-start.7
  16.3 1.2 copy.32
  17.5 17.5 %all-to-all-done.2 = bf16[16,192,128]{2,1,0:T(8,128)(2,1)S(1)} async-done(((bf16[16,192,128]{2,1,0:T(8,128)(2,1)}), bf16[16,192,128]{2,1,0:T(8,128)(2,1)S(1)}, u32[]{:S(2)}, u32[]{:S(2)}) %all-to-all-start.2) | async-done | bytes 786464 | tf_op jit(solution)/shard_map/all_to_all | solution.py:77
  35.0 5.5 %all-to-all-start = ((bf16[16,192,128]{2,1,0:T(8,128)(2,1)}), bf16[16,192,128]{2,1,0:T(8,128)(2,1)S(1)}, u32[]{:S(2)}, u32[]{:S(2)}) async-start(bf16[16,192,128]{2,1,0:T(8,128)(2,1)} %bitcast.1), calls=%async_computation | async-start | bytes 1572864 | tf_op jit(solution)/shard_map/all_to_all | solution.py:76
  40.5 0.0 copy-done.7
  40.5 0.1 copy.33
  40.6 0.1 reshape.317
  40.7 0.1 copy.31
  40.8 2.3 gather_fusion.1
  43.1 16.1 %all-to-all-done = bf16[16,192,128]{2,1,0:T(8,128)(2,1)S(1)} async-done(((bf16[16,192,128]{2,1,0:T(8,128)(2,1)}), bf16[16,192,128]{2,1,0:T(8,128)(2,1)S(1)}, u32[]{:S(2)}, u32[]{:S(2)}) %all-to-all-start) | async-done | bytes 786464 | tf_op jit(solution)/shard_map/all_to_all | solution.py:76
  59.2 2.3 gather_fusion
  61.5 5.1 %select_bitcast_fusion = (bf16[192,16,3,128]{3,0,2,1:T(8,128)(2,1)}, bf16[192,16,3,128]{3,0,2,1:T(8,128)(2,1)}) fusion(bf16[16,3,192,128]{3,2,1,0:T(8,128)(2,1)} %bitcast.170, pred[16,3]{1,0:T(8,128)(4,1)S(1)} %copy.31, bf16[16,3,192,128]{3,2,1,0:T(8,128)(2,1)} %bitcast.171), kind=kLoop, calls=%fused_computation.19 | loop fusion | flops 2359296 | bytes 9437232 | tf_op jit(solution)/shard_map/jit(_take)/select_n | solution.py:88
  66.6 5.6 %all-to-all-start.1 = ((bf16[192,16,3,128]{3,0,2,1:T(8,128)(2,1)}), bf16[192,16,3,128]{3,0,2,1:T(8,128)(2,1)S(1)}, u32[]{:S(2)}, u32[]{:S(2)}) async-start(bf16[192,16,3,128]{3,0,2,1:T(8,128)(2,1)} %get-tuple-element.24), calls=%async_computation.1 | async-start | bytes 4718592 | tf_op jit(solution)/shard_map/all_to_all | solution.py:90
  72.2 0.0 all-reduce.3.cloned.1.call-start
  72.2 0.0 copy-done.8
  72.2 0.6 fusion.42
  74.0 3.8 %pad_maximum_fusion.2 = (bf16[2,128,3072]{1,2,0:T(8,128)(2,1)}, bf16[1,2,128,3072]{2,3,0,1:T(8,128)(2,1)}, bf16[1,2,128,3072]{2,3,1,0:T(8,128)(2,1)}) fusion(bf16[1,128,3072]{1,2,0:T(8,128)(2,1)} %bitcast.11, bf16[1,128,3072]{1,2,0:T(8,128)(2,1)} %bitcast.10, pred[]{:T(512)S(6)} %eq.40, pred[]{:T(512)S(6)} %eq.39), kind=kLoop, calls=%fused_computation.23 | loop fusion | flops 2359296 | bytes 6291458 | tf_op jit(solution)/shard_map/stack | solution.py:74
  77.8 1.3 collective-permute-start.1
  79.1 4.2 %collective-permute-start = (bf16[2,128,3072]{1,2,0:T(8,128)(2,1)}, bf16[2,128,3072]{1,2,0:T(8,128)(2,1)}, u32[]{:S(2)}, u32[]{:S(2)}) collective-permute-start(bf16[2,128,3072]{1,2,0:T(8,128)(2,1)} %get-tuple-element.20), channel_id=1, source_target_pairs={{0,1},{1,2},{2,3},{3,4},{4,5},{5,6},{6,7},{7,8},{8,9},{9,10},{10,1... | collective-permute-start | bytes 4718600 | tf_op jit(solution)/shard_map/ppermute | solution.py:23
  83.3 0.0 all-reduce.3.cloned.1.call-update
  83.3 1.3 copy.88
  84.6 0.7 compare_reduce_fusion.2
  87.1 3.2 %fusion.43 = (f32[24,128]{1,0:T(8,128)S(1)}, f32[24,128,128]{1,2,0:T(8,128)}) fusion(pred[]{:T(512)S(6)} %not.12, bf16[128,3072]{1,0:T(8,128)(2,1)} %param.8, bf16[128,3072]{1,0:T(8,128)(2,1)} %param.7), kind=kOutput, calls=%fused_computation.81 | convolution fusion | flops 101839872 | bytes 3158017 | tf_op jit(solution)/shard_map/bqhd,bkhd->bhqk/dot_general | solution.py:43
  90.3 0.0 collective-permute-done.1
  90.3 0.0 collective-permute-done
  90.3 4.1 %pad_maximum_fusion = bf16[2,384,3072]{1,2,0:T(8,128)(2,1)} fusion(bf16[2,128,3072]{1,2,0:T(8,128)(2,1)} %collective-permute-done.1, bf16[1,128,3072]{1,2,0:T(8,128)(2,1)} %bitcast.11, bf16[1,128,3072]{1,2,0:T(8,128)(2,1)} %bitcast.10, bf16[2,128,3072]{1,2,0:T(8,128)(2,1)} %collective-permute-done), kind=kLoop, calls=%fused_computation.2 | loop fusion | flops 18874368 | bytes 9437184 | tf_op jit(solution)/shard_map/concatenate | solution.py:21
  94.4 6.7 %copy.39 = bf16[2,384,3072]{2,1,0:T(8,128)(2,1)} copy(bf16[2,384,3072]{1,2,0:T(8,128)(2,1)} %pad_maximum_fusion) | data formatting | bytes 9437184 | tf_op jit(solution)/shard_map/concatenate | solution.py:21
  101.1 3.7 %copy.89 = bf16[96,8,24,128]{3,2,1,0:T(8,128)(2,1)S(1)} copy(bf16[96,8,24,128]{3,1,2,0:T(8,128)(2,1)} %bitcast.168) | data formatting | bytes 9437184
  104.8 1.9 fusion.41
  106.7 2.5 copy.85
  109.2 2.4 copy.84
  111.7 3.2 %bitcast_reduce_fusion.2 = (f32[24,128]{1,0:T(8,128)S(1)}, f32[24,128,128]{2,1,0:T(8,128)}) fusion(bf16[1,1,128,24,128]{4,3,2,1,0:T(8,128)(2,1)} %get-tuple-element.15, pred[]{:T(512)S(6)} %and.19, bf16[128,3072]{1,0:T(8,128)(2,1)} %param.7), kind=kOutput, calls=%fused_computation.34 | convolution fusion | flops 101839872 | bytes 3158017 | tf_op jit(solution)/shard_map/bqhd,bkhd->bhqk/dot_general | solution.py:43
  114.9 13.0 %all-to-all-done.1 = bf16[192,16,3,128]{3,0,2,1:T(8,128)(2,1)S(1)} async-done(((bf16[192,16,3,128]{3,0,2,1:T(8,128)(2,1)}), bf16[192,16,3,128]{3,0,2,1:T(8,128)(2,1)S(1)}, u32[]{:S(2)}, u32[]{:S(2)}) %all-to-all-start.1) | async-done | bytes 2359328 | tf_op jit(solution)/shard_map/all_to_all | solution.py:90
  127.9 66.2 %all-to-all-start.3 = ((bf16[192,16,3,128]{3,0,2,1:T(8,128)(2,1)}), bf16[192,16,3,128]{3,0,2,1:T(8,128)(2,1)}, u32[]{:S(2)}, u32[]{:S(2)}) async-start(bf16[192,16,3,128]{3,0,2,1:T(8,128)(2,1)} %get-tuple-element.23), calls=%async_computation.3 | async-start | bytes 4718592 | tf_op jit(solution)/shard_map/all_to_all | solution.py:91
  194.2 3.3 %bitcast_reduce_fusion.3 = (f32[24,128]{1,0:T(8,128)S(1)}, f32[24,128,128]{2,1,0:T(8,128)}) fusion(bf16[1,1,128,24,128]{4,3,2,1,0:T(8,128)(2,1)} %get-tuple-element.16, pred[]{:T(512)S(6)} %and.18, bf16[128,3072]{1,0:T(8,128)(2,1)} %param.7), kind=kOutput, calls=%fused_computation.37 | convolution fusion | flops 101839872 | bytes 3158017 | tf_op jit(solution)/shard_map/bqhd,bkhd->bhqk/dot_general | solution.py:43
  197.5 64.2 %all-reduce.3.cloned.1.call-done = (bf16[1,2,128,3072]{2,3,0,1:T(8,128)(2,1)}, bf16[1,2,128,3072]{2,3,1,0:T(8,128)(2,1)}) async-done(((bf16[1,2,128,3072]{2,3,0,1:T(8,128)(2,1)}, bf16[1,2,128,3072]{2,3,1,0:T(8,128)(2,1)}), (bf16[1,2,128,3072]{2,3,0,1:T(8,128)(2,1)}, bf16[1,2,128,3072]{2,3,1,0:T(8,128)(2,1)})) %all-reduce.3.cloned.1.call-update) | async-done | bytes 3145744 | tf_op jit(solution)/shard_map/psum | solution.py:34
  261.7 2.1 fusion.8
  263.8 0.7 bitcast_reduce_fusion.1
  264.6 0.2 copy.34
  264.8 1.0 bitcast_reduce_fusion
  265.8 0.0 copy-start
  265.8 0.0 copy-start.1
  265.8 0.0 copy-start.2
  265.8 0.5 fusion.3
  266.4 2.1 copy-done.1
  268.5 1.0 copy-done.2
  269.5 1.2 fusion.21
  270.7 0.8 fusion.1
  271.5 0.3 copy-done.6
  271.8 0.4 fusion.29
  272.2 0.7 copy-done.5
  272.9 1.6 fusion.31
  274.6 2.7 fusion.35
  277.3 2.2 fusion.10
  279.4 0.0 all-to-all-done.3
  279.4 2.0 copy.52
  281.4 0.1 copy-done.9
  281.5 0.5 copy-done.10
  282.0 0.5 copy-done.11
  282.5 3.9 %fusion.9 = bf16[1,128,24,128]{1,3,2,0:T(8,128)(2,1)S(1)} fusion(f32[24,128,128,1]{2,1,0,3:T(8,128)S(1)} %copy-done.11, f32[24,128,128]{2,1,0:T(8,128)S(1)} %fusion.29, f32[24,128,128]{2,1,0:T(8,128)S(1)} %copy-done.9, f32[24,128,128]{1,2,0:T(8,128)S(1)} %copy-done.10, bf16[24,128,3,128]{3,1,0,2:T(8,128)(2,1)S(1)} %bitcast.177, ...), kind=kOutput, calls=%fused_computation.25 | convolution fusion | flops 308674560 | bytes 14180352 | tf_op jit(solution)/shard_map/bhqsk,hdbsk->bqhd/dot_general | solution.py:60
  286.4 1.2 copy.61
  (15 shorter events, 0.1 us)
Async XLA Ops:
  6.5 9.7 %copy-start.4 = (bf16[128,3072]{1,0:T(8,128)(2,1)S(1)}, bf16[128,3072]{1,0:T(8,128)(2,1)}, u32[]{:S(2)}) copy-start(bf16[128,3072]{1,0:T(8,128)(2,1)} %param.8) | copy-start | bytes 2359300
  8.9 26.1 %all-to-all-start.2 = ((bf16[16,192,128]{2,1,0:T(8,128)(2,1)}), bf16[16,192,128]{2,1,0:T(8,128)(2,1)S(1)}, u32[]{:S(2)}, u32[]{:S(2)}) async-start(bf16[16,192,128]{2,1,0:T(8,128)(2,1)} %bitcast.29), calls=%async_computation.2 | async-start | bytes 1572864 | tf_op jit(solution)/shard_map/all_to_all | solution.py:77
  16.3 24.2 %copy-start.7 = (s32[16,3]{0,1:T(4,128)S(1)}, s32[16,3]{0,1:T(4,128)}, u32[]{:S(2)}) copy-start(s32[16,3]{0,1:T(4,128)} %param.10) | copy-start | bytes 580
  35.0 24.2 %all-to-all-start = ((bf16[16,192,128]{2,1,0:T(8,128)(2,1)}), bf16[16,192,128]{2,1,0:T(8,128)(2,1)S(1)}, u32[]{:S(2)}, u32[]{:S(2)}) async-start(bf16[16,192,128]{2,1,0:T(8,128)(2,1)} %bitcast.1), calls=%async_computation | async-start | bytes 1572864 | tf_op jit(solution)/shard_map/all_to_all | solution.py:76
  66.6 5.7 %copy-start.8 = (s32[2]{0:T(128)S(1)}, s32[2]{0:T(128)}, u32[]{:S(2)}) copy-start(s32[2]{0:T(128)} %param.11) | copy-start | bytes 28
  66.6 61.3 %all-to-all-start.1 = ((bf16[192,16,3,128]{3,0,2,1:T(8,128)(2,1)}), bf16[192,16,3,128]{3,0,2,1:T(8,128)(2,1)S(1)}, u32[]{:S(2)}, u32[]{:S(2)}) async-start(bf16[192,16,3,128]{3,0,2,1:T(8,128)(2,1)} %get-tuple-element.24), calls=%async_computation.1 | async-start | bytes 4718592 | tf_op jit(solution)/shard_map/all_to_all | solution.py:90
  72.2 189.5 %all-reduce.3.cloned.1.call-start = ((), (), s32[]{:S(2)}) async-start(), calls=%async_computation.4 | async-start | bytes 6291456 | tf_op jit(solution)/shard_map/psum | solution.py:34
  77.8 12.5 %collective-permute-start.1 = (bf16[2,128,3072]{1,2,0:T(8,128)(2,1)}, bf16[2,128,3072]{1,2,0:T(8,128)(2,1)}, u32[]{:S(2)}, u32[]{:S(2)}) collective-permute-start(bf16[2,128,3072]{1,2,0:T(8,128)(2,1)} %get-tuple-element.20), channel_id=1, source_target_pairs={{1,0},{2,1},{3,2},{4,3},{5,4},{6,5},{7,6},{8,7},{9,8},{10,9},{11,1... | collective-permute-start | bytes 4718600 | tf_op jit(solution)/shard_map/ppermute | solution.py:25
  79.1 11.2 %collective-permute-start = (bf16[2,128,3072]{1,2,0:T(8,128)(2,1)}, bf16[2,128,3072]{1,2,0:T(8,128)(2,1)}, u32[]{:S(2)}, u32[]{:S(2)}) collective-permute-start(bf16[2,128,3072]{1,2,0:T(8,128)(2,1)} %get-tuple-element.20), channel_id=1, source_target_pairs={{0,1},{1,2},{2,3},{3,4},{4,5},{5,6},{6,7},{7,8},{8,9},{9,10},{10,1... | collective-permute-start | bytes 4718600 | tf_op jit(solution)/shard_map/ppermute | solution.py:23
  127.9 151.5 %all-to-all-start.3 = ((bf16[192,16,3,128]{3,0,2,1:T(8,128)(2,1)}), bf16[192,16,3,128]{3,0,2,1:T(8,128)(2,1)}, u32[]{:S(2)}, u32[]{:S(2)}) async-start(bf16[192,16,3,128]{3,0,2,1:T(8,128)(2,1)} %get-tuple-element.23), calls=%async_computation.3 | async-start | bytes 4718592 | tf_op jit(solution)/shard_map/all_to_all | solution.py:91
  264.8 1.6 copy-start.3
  265.8 4.9 %copy-start = (f32[24,3,128,128]{3,2,1,0:T(8,128)}, f32[24,3,128,128]{3,2,1,0:T(8,128)S(1)}, u32[]{:S(2)}) copy-start(f32[24,3,128,128]{3,2,1,0:T(8,128)S(1)} %get-tuple-element.36) | copy-start | bytes 14155780
  265.8 2.7 copy-start.1
  265.8 3.7 %copy-start.2 = (f32[24,128,128]{2,1,0:T(8,128)S(1)}, f32[24,128,128]{2,1,0:T(8,128)}, u32[]{:S(2)}) copy-start(f32[24,128,128]{2,1,0:T(8,128)} %get-tuple-element.30) | copy-start | bytes 4718596
  270.7 1.1 copy-start.6
  271.8 1.1 copy-start.5
  279.4 2.1 copy-start.9
  279.4 2.6 copy-start.10
  279.4 3.1 %copy-start.11 = (f32[24,128,128,1]{2,1,0,3:T(8,128)S(1)}, f32[24,128,128,1]{2,1,0,3:T(8,128)}, u32[]{:S(2)}) copy-start(f32[24,128,128,1]{2,1,0,3:T(8,128)} %fusion.10) | copy-start | bytes 4718596
Sparse Core Ops, SparseCore 0:
  83.4 178.2 all-reduce.2
where the time goes:
time: 296 us; the launch traced here: 294 us
  waiting for transfers between devices  111 us (38%)
  starting transfers between devices  90.2 us (30%)
  local copies, waits for them, and re-layouts  36.2 us (12%)
  matrix products  22.4 us (8%)
  other arithmetic  18.3 us (6%)
  between operations  16.7 us (6%)
    all_to_all x1, starting transfers between devices, local(): lax.all_to_all(picked_values, 'seq', split_axis=1, concat_axis=0, tiled=T...  66.2 us
    psum x1, waiting for transfers between devices, broadcast(): return lax.psum(jnp.where(mine, array, jnp.zeros_like(array)), axis)  64.2 us
    unnamed x30, local copies, waits for them, and re-layouts  18.7 us
    all_to_all x1, waiting for transfers between devices, local(): lax.all_to_all(values.T, 'seq', split_axis=0, concat_axis=1, tiled=True)  17.5 us
    all_to_all x1, waiting for transfers between devices, local(): lax.all_to_all(keys.T, 'seq', split_axis=0, concat_axis=1, tiled=True)  16.1 us
    all_to_all x1, waiting for transfers between devices, local(): lax.all_to_all(picked_keys, 'seq', split_axis=1, concat_axis=0, tiled=True)  13 us
    dot_general x5, matrix products, combine_parts(): jnp.einsum(entry[2], probs, entry[1], preferred_element_type=jnp.float32)  10.8 us
    dot_general x3, matrix products, local_scores(): jnp.einsum('bqhd,bkhd->bhqk', query_blocks, key_part, preferred_element_t...  9.77 us
  transfers between devices with their start and end apart: 7, of which 4 were waited for; matrix products, arithmetic and copies ran while one was open for 19% of the time, Pallas kernels for 0%

commit v1 on v0

v1 whole, which is shorter than its diff:
```python
import functools

import jax
import jax.numpy as jnp
from jax import lax
from jax.experimental import pallas as pl
from jax.experimental.pallas import tpu as pltpu
from jax.sharding import PartitionSpec as P

HEADS = 24
HEAD_DIM = 128
BLOCK = 128
GLOBALS = 2
RANDOMS = 3
LOCAL_HEADS = 3
GROUPS = HEADS // LOCAL_HEADS
MESH = pl.DeviceIdType.MESH
NEG = -1e30


def kernel(ranks, rand_ref, glob_ref, q_hbm, k_hbm, v_hbm, out_hbm, *scratch):
    qs, ks, vs, os = (scratch[3 * i : 3 * i + 3] for i in range(4))
    (send_sem, recv_sem, fwd_send, fwd_recv, own_sem, out_send, out_recv, out_own) = scratch[12:]
    rollout = lax.axis_index("groups")
    me = lax.axis_index("seq")
    group, rank = lax.div(me, ranks), lax.rem(me, ranks)
    blocks = ranks * GROUPS

    def peer(j):
        return lax.rem(group + j, GROUPS)

    def sibling(i):
        return group * ranks + lax.rem(rank + i, ranks)

    def device(index):
        return (rollout, index)

    barrier = pltpu.get_barrier_semaphore()

    @pl.loop(1, GROUPS)
    def _(j):
        pl.semaphore_signal(barrier, inc=1, device_id=device(peer(j) * ranks + rank), device_id_type=MESH)

    @pl.loop(1, ranks)
    def _(i):
        pl.semaphore_signal(barrier, inc=1, device_id=device(sibling(i)), device_id_type=MESH)

    pl.semaphore_wait(barrier, GROUPS - 1 + ranks - 1)

    sources = (q_hbm, k_hbm, v_hbm)

    def columns(owner, h):
        start = pl.multiple_of((owner * LOCAL_HEADS + h) * HEAD_DIM, HEAD_DIM)
        return pl.ds(start, HEAD_DIM)

    def slab(t, h, owner_group):
        if t == 0:
            return qs[h].at[owner_group]
        return (ks, vs)[t - 1][h].at[owner_group * ranks + rank]

    def send(t, h, j):
        return pltpu.make_async_remote_copy(
            src_ref=sources[t].at[:, columns(peer(j), h)],
            dst_ref=slab(t, h, group),
            send_sem=send_sem.at[h, t, j],
            recv_sem=recv_sem.at[h, t, j],
            device_id=device(peer(j) * ranks + rank),
            device_id_type=MESH,
        )

    def received(t, h, j):
        here = slab(t, h, lax.rem(group + GROUPS - j, GROUPS))
        return pltpu.make_async_remote_copy(
            src_ref=here,
            dst_ref=here,
            send_sem=send_sem.at[h, t, j],
            recv_sem=recv_sem.at[h, t, j],
            device_id=device(peer(j) * ranks + rank),
            device_id_type=MESH,
        )

    def own(t, h):
        return pltpu.make_async_copy(
            sources[t].at[:, columns(group, h)], slab(t, h, group), own_sem.at[h, t]
        )

    def forward(t, h, j, i):
        here = slab(t, h, lax.rem(group + GROUPS - j, GROUPS))
        return pltpu.make_async_remote_copy(
            src_ref=here,
            dst_ref=here,
            send_sem=fwd_send.at[h, t - 1, i, j],
            recv_sem=fwd_recv.at[h, t - 1, i, j],
            device_id=device(sibling(i)),
            device_id_type=MESH,
        )

    def forwarded(t, h, j, i):
        block = lax.rem(group + GROUPS - j, GROUPS) * ranks + lax.rem(rank + ranks - i, ranks)
        here = (ks, vs)[t - 1][h].at[block]
        return pltpu.make_async_remote_copy(
            src_ref=here,
            dst_ref=here,
            send_sem=fwd_send.at[h, t - 1, i, j],
            recv_sem=fwd_recv.at[h, t - 1, i, j],
            device_id=device(sibling(i)),
            device_id_type=MESH,
        )

    def send_out(h, j):
        return pltpu.make_async_remote_copy(
            src_ref=os[h].at[peer(j)],
            dst_ref=out_hbm.at[:, columns(group, h)],
            send_sem=out_send.at[h, j],
            recv_sem=out_recv.at[h, j],
            device_id=device(peer(j) * ranks + rank),
            device_id_type=MESH,
        )

    def out_received(h, j):
        owner = lax.rem(group + GROUPS - j, GROUPS)
        return pltpu.make_async_remote_copy(
            src_ref=os[h].at[peer(j)],
            dst_ref=out_hbm.at[:, columns(owner, h)],
            send_sem=out_send.at[h, j],
            recv_sem=out_recv.at[h, j],
            device_id=device(peer(j) * ranks + rank),
            device_id_type=MESH,
        )

    def out_local(h):
        return pltpu.make_async_copy(os[h].at[group], out_hbm.at[:, columns(group, h)], out_own.at[h])

    for h in range(LOCAL_HEADS):
        for t in (1, 2, 0):
            own(t, h).start()

        @pl.loop(1, GROUPS)
        def _(j):
            for t in (1, 2, 0):
                send(t, h, j).start()

    def attend(h, slot):
        block = slot * ranks + rank
        g0, g1 = glob_ref[0], glob_ref[1]

        def bias(b, inside):
            ok = inside & (b != g0) & (b != g1)
            return jnp.where(ok, jnp.float32(0.0), jnp.float32(NEG))

        ids = [
            jnp.maximum(block - 1, 0),
            block,
            jnp.minimum(block + 1, blocks - 1),
            g0,
            g1,
        ] + [rand_ref[block, r] for r in range(RANDOMS)]
        biases = [
            bias(block - 1, block >= 1),
            bias(block, block >= 0),
            bias(block + 1, block + 1 < blocks),
        ]
        query = qs[h][slot]
        key = jnp.concatenate([ks[h][i] for i in ids], axis=0)
        value = jnp.concatenate([vs[h][i] for i in ids], axis=0)
        scores = lax.dot_general(
            query, key, (((1,), (1,)), ((), ())), preferred_element_type=jnp.float32
        ) * (HEAD_DIM ** -0.5)
        parts = [scores[:, n * BLOCK : (n + 1) * BLOCK] for n in range(len(ids))]
        parts = [part + biases[n] if n < 3 else part for n, part in enumerate(parts)]
        top = jnp.max(functools.reduce(jnp.maximum, parts), axis=1, keepdims=True)
        powers = [jnp.exp(part - top) for part in parts]
        total = jnp.sum(functools.reduce(jnp.add, powers), axis=1, keepdims=True)
        inverse = 1.0 / total
        probs = jnp.concatenate([(power * inverse).astype(jnp.bfloat16) for power in powers], axis=1)
        result = lax.dot_general(
            probs, value, (((1,), (0,)), ((), ())), preferred_element_type=jnp.float32
        )
        os[h][slot] = result.astype(jnp.bfloat16)

    for h in range(LOCAL_HEADS):
        for t in (1, 2):
            own(t, h).wait()

            @pl.loop(1, ranks)
            def _(i):
                forward(t, h, 0, i).start()

        @pl.loop(1, GROUPS)
        def _(j):
            for t in (1, 2):
                received(t, h, j).wait_recv()

                @pl.loop(1, ranks)
                def _(i):
                    forward(t, h, j, i).start()

        own(0, h).wait()

        @pl.loop(1, GROUPS)
        def _(j):
            received(0, h, j).wait_recv()

        @pl.loop(1, ranks)
        def _(i):
            @pl.loop(0, GROUPS)
            def _(j):
                for t in (1, 2):
                    forwarded(t, h, j, i).wait_recv()

        @pl.loop(1, GROUPS)
        def _(j):
            attend(h, peer(j))
            send_out(h, j).start()

        attend(h, group)
        out_local(h).start()

    for h in range(LOCAL_HEADS):
        out_local(h).wait()

        @pl.loop(1, GROUPS)
        def _(j):
            for t in range(3):
                send(t, h, j).wait_send()
            send_out(h, j).wait_send()
            out_received(h, j).wait_recv()

        @pl.loop(1, ranks)
        def _(i):
            @pl.loop(0, GROUPS)
            def _(j):
                for t in (1, 2):
                    forward(t, h, j, i).wait_send()


def local(queries, keys, values, rand_blocks, global_ids):
    seq = lax.axis_size("seq")
    ranks = seq // GROUPS
    blocks = rand_blocks.shape[0]
    assert queries.shape[0] == BLOCK and blocks == seq and seq % GROUPS == 0
    tile = (BLOCK, HEAD_DIM)
    anywhere = pl.BlockSpec(memory_space=pl.ANY)
    scalars = pl.BlockSpec(memory_space=pltpu.SMEM)
    dma = pltpu.SemaphoreType.DMA
    return pl.pallas_call(
        functools.partial(kernel, ranks),
        out_shape=jax.ShapeDtypeStruct(queries.shape, jnp.bfloat16),
        in_specs=[scalars, scalars, anywhere, anywhere, anywhere],
        out_specs=anywhere,
        scratch_shapes=[pltpu.VMEM((GROUPS,) + tile, jnp.bfloat16)] * LOCAL_HEADS
        + [pltpu.VMEM((blocks,) + tile, jnp.bfloat16)] * (2 * LOCAL_HEADS)
        + [pltpu.VMEM((GROUPS,) + tile, jnp.bfloat16)] * LOCAL_HEADS
        + [
            dma((LOCAL_HEADS, 3, GROUPS)),
            dma((LOCAL_HEADS, 3, GROUPS)),
            dma((LOCAL_HEADS, 2, ranks, GROUPS)),
            dma((LOCAL_HEADS, 2, ranks, GROUPS)),
            dma((LOCAL_HEADS, 3)),
            dma((LOCAL_HEADS, GROUPS)),
            dma((LOCAL_HEADS, GROUPS)),
            dma((LOCAL_HEADS,)),
        ],
        compiler_params=pltpu.CompilerParams(
            collective_id=0, has_side_effects=True, vmem_limit_bytes=48 << 20
        ),
    )(rand_blocks, global_ids, queries, keys, values)


def solution(mesh):
    placed = (
        P(("groups", "seq"), None),
        P(("groups", "seq"), None),
        P(("groups", "seq"), None),
        P("groups", None),
        P("groups"),
    )
    return jax.shard_map(
        local, mesh=mesh, in_specs=placed, out_specs=P(("groups", "seq"), None), check_vma=False
    )
```

time: 296 us -> 83.1 us (0.28)
  waiting for transfers between devices: 111 us -> 0 us
  starting transfers between devices: 90.2 us -> 0 us
  Pallas kernels: 0 us -> 77.8 us
  local copies, waits for them, and re-layouts: 36.2 us -> 5.06 us
  matrix products: 22.4 us -> 0 us
  other arithmetic: 18.3 us -> 0 us
  between operations: 16.7 us -> 0.01 us
    all_to_all x4 -> x0, starting transfers between devices: 84.7 us -> none  [the longest x1 66.2 us: local(): lax.all_to_all(picked_values, 'seq', split_axis=1, concat_axis=0, tiled=T...]
    pallas_call x0 -> x1, Pallas kernels: none -> 77.8 us  [local(): pl.pallas_call(functools.partial(kernel, ranks), out_shape=jax.ShapeDtype...]
    psum x1 -> x0, waiting for transfers between devices: 64.2 us -> none  [broadcast(): return lax.psum(jnp.where(mine, array, jnp.zeros_like(array)), axis)]
    all_to_all x4 -> x0, waiting for transfers between devices: 46.5 us -> none  [the longest x1 17.5 us: local(): lax.all_to_all(values.T, 'seq', split_axis=0, concat_axis=1, tiled=True)]
    dot_general x10 -> x0, matrix products: 22.4 us -> none  [the longest x5 10.8 us: combine_parts(): jnp.einsum(entry[2], probs, entry[1], preferred_element_type=jnp.float32)]
    unnamed x30 -> x10, local copies, waits for them, and re-layouts: 18.7 us -> 5.06 us
    concatenate x1 -> x0, local copies, waits for them, and re-layouts: 6.71 us -> none  [padded_2(): jnp.concatenate([lax.ppermute(tail, axis, [(i, (i + 1) % count) for i in...]
    another operation x2 -> x0, other arithmetic: 5.88 us -> none  [the longest x1 3.77 us: local(): stacked = jnp.stack([keys, values])]
  transfers between devices with their start and end apart: 7 -> 0, of which waited for: 4 -> 0; matrix products, arithmetic and copies ran while one was open for 19% -> 0% of each run, Pallas kernels for 0% -> 0%
where the time goes in v1:
time: 83.1 us; the launch traced here: 82.9 us
  Pallas kernels  77.8 us (94%)
  local copies, waits for them, and re-layouts  5.06 us (6%)
    pallas_call x1, Pallas kernels, local(): pl.pallas_call(functools.partial(kernel, ranks), out_shape=jax.ShapeDtype...  77.8 us
    unnamed x10, local copies, waits for them, and re-layouts  5.06 us

profile of v1, /device:TPU:0, one launch (start us, length us, event | category | flops | bytes accessed | tf_op | source)
XLA Modules:
  0.0 82.9 jit_solution(2958023656846394976)
XLA Ops:
  0.0 0.0 copy-start.3
  0.0 0.8 copy.6.rand_ref
  0.8 0.0 copy-done.3
  0.8 0.0 copy-start
  0.8 1.1 %copy-done = bf16[128,3072]{1,0:T(8,128)(2,1)S(1)} copy-done((bf16[128,3072]{1,0:T(8,128)(2,1)S(1)}, bf16[128,3072]{1,0:T(8,128)(2,1)}, u32[]{:S(2)}) %copy-start) | copy-done | bytes 786456
  1.9 0.0 copy-start.1
  1.9 1.1 %copy-done.1 = bf16[128,3072]{1,0:T(8,128)(2,1)S(1)} copy-done((bf16[128,3072]{1,0:T(8,128)(2,1)S(1)}, bf16[128,3072]{1,0:T(8,128)(2,1)}, u32[]{:S(2)}) %copy-start.1) | copy-done | bytes 786456
  3.0 0.0 copy-start.2
  3.0 1.1 %copy-done.2 = bf16[128,3072]{1,0:T(8,128)(2,1)S(1)} copy-done((bf16[128,3072]{1,0:T(8,128)(2,1)S(1)}, bf16[128,3072]{1,0:T(8,128)(2,1)}, u32[]{:S(2)}) %copy-start.2) | copy-done | bytes 786456
  4.2 77.8 %shard_map.55 = bf16[128,3072]{1,0:T(8,128)(2,1)S(1)} custom-call(s32[16,3]{1,0:T(8,128)S(1)} %copy.6.rand_ref, s32[2]{0:T(128)S(1)} %copy-done.3, bf16[128,3072]{1,0:T(8,128)(2,1)S(1)} %copy-done, bf16[128,3072]{1,0:T(8,128)(2,1)S(1)} %copy-done.1, bf16[128,3072]{1,0:T(8,128)(2,1)S(1)} %copy-done.2), custom_call_target="tpu_custom_call" | custom-call | tf_op jit(solution)/shard_map/pallas_call | solution.py:246
  82.0 0.9 %copy.8 = bf16[128,3072]{1,0:T(8,128)(2,1)} copy(bf16[128,3072]{1,0:T(8,128)(2,1)S(1)} %shard_map.55) | data formatting | bytes 1572864
Async XLA Ops:
  0.0 0.8 copy-start.3
  0.8 1.1 %copy-start = (bf16[128,3072]{1,0:T(8,128)(2,1)S(1)}, bf16[128,3072]{1,0:T(8,128)(2,1)}, u32[]{:S(2)}) copy-start(bf16[128,3072]{1,0:T(8,128)(2,1)} %q_hbm.1) | copy-start | bytes 2359300
  1.9 1.1 %copy-start.1 = (bf16[128,3072]{1,0:T(8,128)(2,1)S(1)}, bf16[128,3072]{1,0:T(8,128)(2,1)}, u32[]{:S(2)}) copy-start(bf16[128,3072]{1,0:T(8,128)(2,1)} %k_hbm.1) | copy-start | bytes 2359300
  3.0 1.1 %copy-start.2 = (bf16[128,3072]{1,0:T(8,128)(2,1)S(1)}, bf16[128,3072]{1,0:T(8,128)(2,1)}, u32[]{:S(2)}) copy-start(bf16[128,3072]{1,0:T(8,128)(2,1)} %v_hbm.1) | copy-start | bytes 2359300

commit v2 on v1

--- a/solution.py
+++ b/solution.py
@@ -154,7 +154,7 @@
             jnp.minimum(block + 1, blocks - 1),
             g0,
             g1,
-        ] + [rand_ref[block, r] for r in range(RANDOMS)]
+        ] + [rand_ref[r, block] for r in range(RANDOMS)]
         biases = [
             bias(block - 1, block >= 1),
             bias(block, block >= 0),
@@ -240,6 +240,10 @@
     blocks = rand_blocks.shape[0]
     assert queries.shape[0] == BLOCK and blocks == seq and seq % GROUPS == 0
     tile = (BLOCK, HEAD_DIM)
+    operands = [
+        pltpu.with_memory_space_constraint(x, pltpu.MemorySpace.HBM)
+        for x in (rand_blocks.T, global_ids, queries, keys, values)
+    ]
     anywhere = pl.BlockSpec(memory_space=pl.ANY)
     scalars = pl.BlockSpec(memory_space=pltpu.SMEM)
     dma = pltpu.SemaphoreType.DMA
@@ -262,9 +266,9 @@
             dma((LOCAL_HEADS,)),
         ],
         compiler_params=pltpu.CompilerParams(
-            collective_id=0, has_side_effects=True, vmem_limit_bytes=48 << 20
+            collective_id=0, has_side_effects=True, vmem_limit_bytes=40 << 20
         ),
-    )(rand_blocks, global_ids, queries, keys, values)
+    )(*operands)
 
 
 def solution(mesh):

time: 83.1 us -> 79 us (0.951)
  local copies, waits for them, and re-layouts: 5.06 us -> 0.88 us
    unnamed x10 -> x1, local copies, waits for them, and re-layouts: 5.06 us -> 0.88 us
where the time goes in v2:
time: 79 us; the launch traced here: 78.8 us
  Pallas kernels  78 us (99%)
  local copies, waits for them, and re-layouts  0.88 us (1%)
    pallas_call x1, Pallas kernels, local(): pl.pallas_call(functools.partial(kernel, ranks), out_shape=jax.ShapeDtype...  78 us

profile of v2, /device:TPU:0, one launch (start us, length us, event | category | flops | bytes accessed | tf_op | source)
XLA Modules:
  0.0 78.8 jit_solution(14227070608065808537)
XLA Ops:
  0.0 78.0 %shard_map.55 = bf16[128,3072]{1,0:T(8,128)(2,1)S(1)} custom-call(s32[3,16]{1,0:T(4,128)} %bitcast.1, s32[2]{0:T(128)} %glob_ref.1, bf16[128,3072]{1,0:T(8,128)(2,1)} %q_hbm.1, bf16[128,3072]{1,0:T(8,128)(2,1)} %k_hbm.1, bf16[128,3072]{1,0:T(8,128)(2,1)} %v_hbm.1), custom_call_target="tpu_custom_call" | custom-call | tf_op jit(solution)/shard_map/pallas_call | solution.py:250
  78.0 0.9 %copy.7 = bf16[128,3072]{1,0:T(8,128)(2,1)} copy(bf16[128,3072]{1,0:T(8,128)(2,1)S(1)} %shard_map.55) | data formatting | bytes 1572864

commit v3 on v2

v3 whole, which is shorter than its diff:
```python
import functools

import jax
import jax.numpy as jnp
from jax import lax
from jax.experimental import pallas as pl
from jax.experimental.pallas import tpu as pltpu
from jax.sharding import PartitionSpec as P

HEADS = 24
HEAD_DIM = 128
BLOCK = 128
GLOBALS = 2
RANDOMS = 3
LOCAL_HEADS = 3
GROUPS = HEADS // LOCAL_HEADS
MESH = pl.DeviceIdType.MESH
NEG = -1e30


def kernel(ranks, rand_ref, glob_ref, q_hbm, k_hbm, v_hbm, out_hbm, *scratch):
    qs, ks, vs, os = (scratch[3 * i : 3 * i + 3] for i in range(4))
    (send_sem, recv_sem, fwd_send, fwd_recv, own_sem, out_send, out_recv, out_own, late_sem) = scratch[12:]
    rollout = lax.axis_index("groups")
    me = lax.axis_index("seq")
    group, rank = lax.div(me, ranks), lax.rem(me, ranks)
    blocks = ranks * GROUPS

    def for_peers(body):
        @pl.loop(1, GROUPS)
        def _(j):
            body(lax.rem(group + j, GROUPS))

    def sibling(i):
        return group * ranks + lax.rem(rank + i, ranks)

    def device(index):
        return (rollout, index)

    barrier = pltpu.get_barrier_semaphore()

    late_from = GROUPS - GROUPS // 4
    late = group >= late_from

    @for_peers
    def _(p):
        @pl.when(jnp.logical_not(late) | (p >= late_from))
        def _():
            pl.semaphore_signal(barrier, inc=1, device_id=device(p * ranks + rank), device_id_type=MESH)

    @pl.loop(1, ranks)
    def _(i):
        pl.semaphore_signal(barrier, inc=1, device_id=device(sibling(i)), device_id_type=MESH)

    pl.semaphore_wait(barrier, jnp.where(late, GROUPS, late_from) - 1 + ranks - 1)

    @pl.when(late)
    def _():
        @pl.loop(0, late_from)
        def _(p):
            pl.semaphore_signal(late_sem, inc=1, device_id=device(p * ranks + rank), device_id_type=MESH)

    sources = (q_hbm, k_hbm, v_hbm)

    def columns(owner, h):
        start = pl.multiple_of((owner * LOCAL_HEADS + h) * HEAD_DIM, HEAD_DIM)
        return pl.ds(start, HEAD_DIM)

    def slab(t, h, owner_group):
        if t == 0:
            return qs[h].at[owner_group]
        return (ks, vs)[t - 1][h].at[owner_group * ranks + rank]

    def send(t, h, p):
        return pltpu.make_async_remote_copy(
            src_ref=sources[t].at[:, columns(p, h)],
            dst_ref=slab(t, h, group),
            send_sem=send_sem.at[h, t, p],
            recv_sem=recv_sem.at[h, t, group],
            device_id=device(p * ranks + rank),
            device_id_type=MESH,
        )

    def received(t, h, p):
        here = slab(t, h, p)
        return pltpu.make_async_remote_copy(
            src_ref=here,
            dst_ref=here,
            send_sem=send_sem.at[h, t, p],
            recv_sem=recv_sem.at[h, t, p],
            device_id=device(p * ranks + rank),
            device_id_type=MESH,
        )

    def own(t, h):
        return pltpu.make_async_copy(
            sources[t].at[:, columns(group, h)], slab(t, h, group), own_sem.at[h, t]
        )

    def forward(t, h, p, i):
        here = slab(t, h, p)
        return pltpu.make_async_remote_copy(
            src_ref=here,
            dst_ref=here,
            send_sem=fwd_send.at[h, t - 1, i, p],
            recv_sem=fwd_recv.at[h, t - 1, i, p],
            device_id=device(sibling(i)),
            device_id_type=MESH,
        )

    def forwarded(t, h, p, i):
        here = (ks, vs)[t - 1][h].at[p * ranks + lax.rem(rank + ranks - i, ranks)]
        return pltpu.make_async_remote_copy(
            src_ref=here,
            dst_ref=here,
            send_sem=fwd_send.at[h, t - 1, i, p],
            recv_sem=fwd_recv.at[h, t - 1, i, p],
            device_id=device(sibling(i)),
            device_id_type=MESH,
        )

    def send_out(h, p):
        return pltpu.make_async_remote_copy(
            src_ref=os[h].at[p],
            dst_ref=out_hbm.at[:, columns(group, h)],
            send_sem=out_send.at[h, p],
            recv_sem=out_recv.at[h, group],
            device_id=device(p * ranks + rank),
            device_id_type=MESH,
        )

    def out_received(h, p):
        return pltpu.make_async_remote_copy(
            src_ref=os[h].at[p],
            dst_ref=out_hbm.at[:, columns(p, h)],
            send_sem=out_send.at[h, p],
            recv_sem=out_recv.at[h, p],
            device_id=device(p * ranks + rank),
            device_id_type=MESH,
        )

    def out_local(h):
        return pltpu.make_async_copy(os[h].at[group], out_hbm.at[:, columns(group, h)], out_own.at[h])

    for h in range(LOCAL_HEADS):
        @for_peers
        def _(p):
            @pl.when(late | (p < late_from) | (h > 0))
            def _():
                for t in (1, 2, 0):
                    send(t, h, p).start()

        if h == 0:
            @pl.when(jnp.logical_not(late))
            def _():
                pl.semaphore_wait(late_sem, GROUPS - late_from)

                @pl.loop(late_from, GROUPS)
                def _(p):
                    for t in (1, 2, 0):
                        send(t, h, p).start()

        for t in (1, 2, 0):
            own(t, h).start()

    def attend(h, slot):
        block = slot * ranks + rank
        g0, g1 = glob_ref[0], glob_ref[1]

        def bias(b, inside):
            ok = inside & (b != g0) & (b != g1)
            return jnp.where(ok, jnp.float32(0.0), jnp.float32(NEG))

        ids = [
            jnp.maximum(block - 1, 0),
            block,
            jnp.minimum(block + 1, blocks - 1),
            g0,
            g1,
        ] + [rand_ref[r, block] for r in range(RANDOMS)]
        biases = [
            bias(block - 1, block >= 1),
            bias(block, block >= 0),
            bias(block + 1, block + 1 < blocks),
        ]
        query = qs[h][slot]
        key = jnp.concatenate([ks[h][i] for i in ids], axis=0)
        value = jnp.concatenate([vs[h][i] for i in ids], axis=0)
        scores = lax.dot_general(
            query, key, (((1,), (1,)), ((), ())), preferred_element_type=jnp.float32
        ) * (HEAD_DIM ** -0.5)
        parts = [scores[:, n * BLOCK : (n + 1) * BLOCK] for n in range(len(ids))]
        parts = [part + biases[n] if n < 3 else part for n, part in enumerate(parts)]
        top = jnp.max(functools.reduce(jnp.maximum, parts), axis=1, keepdims=True)
        powers = [jnp.exp(part - top) for part in parts]
        total = jnp.sum(functools.reduce(jnp.add, powers), axis=1, keepdims=True)
        inverse = 1.0 / total
        probs = jnp.concatenate([(power * inverse).astype(jnp.bfloat16) for power in powers], axis=1)
        result = lax.dot_general(
            probs, value, (((1,), (0,)), ((), ())), preferred_element_type=jnp.float32
        )
        os[h][slot] = result.astype(jnp.bfloat16)

    for h in range(LOCAL_HEADS):
        for t in (1, 2):
            own(t, h).wait()

            @pl.loop(1, ranks)
            def _(i):
                forward(t, h, group, i).start()

        @for_peers
        def _(p):
            for t in (1, 2):
                received(t, h, p).wait_recv()

                @pl.loop(1, ranks)
                def _(i):
                    forward(t, h, p, i).start()

        own(0, h).wait()

        @for_peers
        def _(p):
            received(0, h, p).wait_recv()

        @pl.loop(1, ranks)
        def _(i):
            @pl.loop(0, GROUPS)
            def _(p):
                for t in (1, 2):
                    forwarded(t, h, p, i).wait_recv()

        @pl.loop(0, GROUPS)
        def _(p):
            attend(h, p)

            @pl.when(p != group)
            def _():
                send_out(h, p).start()

        out_local(h).start()

    for h in range(LOCAL_HEADS):
        out_local(h).wait()

        @for_peers
        def _(p):
            for t in range(3):
                send(t, h, p).wait_send()
            send_out(h, p).wait_send()
            out_received(h, p).wait_recv()

        @pl.loop(1, ranks)
        def _(i):
            @pl.loop(0, GROUPS)
            def _(p):
                for t in (1, 2):
                    forward(t, h, p, i).wait_send()


def local(queries, keys, values, rand_blocks, global_ids):
    seq = lax.axis_size("seq")
    ranks = seq // GROUPS
    blocks = rand_blocks.shape[0]
    assert queries.shape[0] == BLOCK and blocks == seq and seq % GROUPS == 0
    tile = (BLOCK, HEAD_DIM)
    sources = [pltpu.with_memory_space_constraint(x, pltpu.MemorySpace.HBM) for x in (rand_blocks.T, global_ids, queries, keys, values)]
    anywhere = pl.BlockSpec(memory_space=pl.ANY)
    scalars = pl.BlockSpec(memory_space=pltpu.SMEM)
    dma = pltpu.SemaphoreType.DMA
    return pl.pallas_call(
        functools.partial(kernel, ranks),
        out_shape=jax.ShapeDtypeStruct(queries.shape, jnp.bfloat16),
        in_specs=[scalars, scalars, anywhere, anywhere, anywhere],
        out_specs=anywhere,
        scratch_shapes=[pltpu.VMEM((GROUPS,) + tile, jnp.bfloat16)] * LOCAL_HEADS
        + [pltpu.VMEM((blocks,) + tile, jnp.bfloat16)] * (2 * LOCAL_HEADS)
        + [pltpu.VMEM((GROUPS,) + tile, jnp.bfloat16)] * LOCAL_HEADS
        + [
            dma((LOCAL_HEADS, 3, GROUPS)),
            dma((LOCAL_HEADS, 3, GROUPS)),
            dma((LOCAL_HEADS, 2, ranks, GROUPS)),
            dma((LOCAL_HEADS, 2, ranks, GROUPS)),
            dma((LOCAL_HEADS, 3)),
            dma((LOCAL_HEADS, GROUPS)),
            dma((LOCAL_HEADS, GROUPS)),
            dma((LOCAL_HEADS,)),
            pltpu.SemaphoreType.REGULAR,
        ],
        compiler_params=pltpu.CompilerParams(
            collective_id=0, has_side_effects=True, vmem_limit_bytes=40 << 20
        ),
    )(*sources)


def solution(mesh):
    placed = (
        P(("groups", "seq"), None),
        P(("groups", "seq"), None),
        P(("groups", "seq"), None),
        P("groups", None),
        P("groups"),
    )
    return jax.shard_map(
        local, mesh=mesh, in_specs=placed, out_specs=P(("groups", "seq"), None), check_vma=False
    )
```

time: 79 us -> 78.2 us (0.990)
  Pallas kernels: 78 us -> 77.1 us
    pallas_call x1, Pallas kernels: 78 us -> 77.1 us  [local(): pl.pallas_call(functools.partial(kernel, ranks), out_shape=jax.ShapeDtype...]
where the time goes in v3:
time: 78.2 us; the launch traced here: 78 us
  Pallas kernels  77.1 us (99%)
  local copies, waits for them, and re-layouts  0.88 us (1%)
    pallas_call x1, Pallas kernels, local(): pl.pallas_call(functools.partial(kernel, ranks), out_shape=jax.ShapeDtype...  77.1 us

profile of v3, /device:TPU:0, one launch (start us, length us, event | category | flops | bytes accessed | tf_op | source)
XLA Modules:
  0.0 78.0 jit_solution(6120600366591887855)
XLA Ops:
  0.0 77.1 %shard_map.55 = bf16[128,3072]{1,0:T(8,128)(2,1)S(1)} custom-call(s32[3,16]{1,0:T(4,128)} %bitcast.1, s32[2]{0:T(128)} %glob_ref.1, bf16[128,3072]{1,0:T(8,128)(2,1)} %q_hbm.1, bf16[128,3072]{1,0:T(8,128)(2,1)} %k_hbm.1, bf16[128,3072]{1,0:T(8,128)(2,1)} %v_hbm.1), custom_call_target="tpu_custom_call" | custom-call | tf_op jit(solution)/shard_map/pallas_call | solution.py:272
  77.1 0.9 %copy.7 = bf16[128,3072]{1,0:T(8,128)(2,1)} copy(bf16[128,3072]{1,0:T(8,128)(2,1)S(1)} %shard_map.55) | data formatting | bytes 1572864

commit v4 on v3

--- a/solution.py
+++ b/solution.py
@@ -27,9 +27,9 @@
     blocks = ranks * GROUPS
 
     def for_peers(body):
-        @pl.loop(1, GROUPS)
+        @pl.loop(0, GROUPS - 1)
         def _(j):
-            body(lax.rem(group + j, GROUPS))
+            body(j + jnp.where(j >= group, 1, 0))
 
     def sibling(i):
         return group * ranks + lax.rem(rank + i, ranks)

time: 78.2 us -> 78.1 us (level)
  no operation moved by 1% of the time
where the time goes in v4:
time: 78.1 us; the launch traced here: 77.9 us
  Pallas kernels  77 us (99%)
  local copies, waits for them, and re-layouts  0.88 us (1%)
    pallas_call x1, Pallas kernels, local(): pl.pallas_call(functools.partial(kernel, ranks), out_shape=jax.ShapeDtype...  77 us

profile of v4, /device:TPU:0, one launch (start us, length us, event | category | flops | bytes accessed | tf_op | source)
XLA Modules:
  0.0 77.9 jit_solution(13886335454130184850)
XLA Ops:
  0.0 77.0 %shard_map.55 = bf16[128,3072]{1,0:T(8,128)(2,1)S(1)} custom-call(s32[3,16]{1,0:T(4,128)} %bitcast.1, s32[2]{0:T(128)} %glob_ref.1, bf16[128,3072]{1,0:T(8,128)(2,1)} %q_hbm.1, bf16[128,3072]{1,0:T(8,128)(2,1)} %k_hbm.1, bf16[128,3072]{1,0:T(8,128)(2,1)} %v_hbm.1), custom_call_target="tpu_custom_call" | custom-call | tf_op jit(solution)/shard_map/pallas_call | solution.py:272
  77.0 0.9 %copy.7 = bf16[128,3072]{1,0:T(8,128)(2,1)} copy(bf16[128,3072]{1,0:T(8,128)(2,1)S(1)} %shard_map.55) | data formatting | bytes 1572864
